TPU v7x, 128 devices: a whole 4x4x4 slice. The times are simulated.
128 devices in a mesh: ctx: 32 (over y, z, core), exp: 4 (over x).
Axes of the slice: x: 4, y: 4, z: 4, core: 2. Of those that a mesh axis runs over, the one named last changes fastest.
Arguments:
- inputs: bfloat16 [4096, 4096], P('ctx', 'exp'), may hold values from -6 to 6
- gate_input: bfloat16 [4096, 4096], P('ctx', 'exp')
- b_proj: bfloat16 [4096, 128], P('ctx'), may hold values from -0.5 to 0.5
- c_proj: bfloat16 [4096, 128], P('ctx'), may hold values from -6 to 6
- step_size: float32 [64, 4096], P('exp', 'ctx'), may hold values from 0.03 to 0.3
- decay_rate: float32 [64, 4096], P('exp', 'ctx'), as said below
- skip_gain: float32 [64], P('exp'), may hold values from 0.5 to 2
- start_state: float32 [64, 64, 128], P('exp'), may hold values from -3 to 3
- norm_gain: float32 [4096], P('exp'), may hold values from 0.5 to 1.5
- out_proj: bfloat16 [4096, 4096], P('exp', 'ctx'), may hold values from -0.09375 to 0.09375
- residual: bfloat16 [4096, 4096], P('ctx'), may hold values from -6 to 6
- moe_gain: float32 [4096], replicated, may hold values from 0.5 to 1.5
- w_gate: bfloat16 [32, 4096, 3584], P('ctx', None, 'exp'), may hold values from -0.09375 to 0.09375
- w_up: bfloat16 [32, 4096, 3584], P('ctx', None, 'exp'), may hold values from -0.09375 to 0.09375
- w_down: bfloat16 [32, 3584, 4096], P('ctx', 'exp'), may hold values from -0.0625 to 0.0625
- route_ids: int32 [4096, 2], P('ctx'), may hold values from 0 to 15, all different within a row; in each aligned block of 32 rows (0 to 31, 32 to 63, ...) at most 8 rows name the same one
- route_gates: float32 [4096, 2], P('ctx'), may hold values from 0.3 to 1
Outputs:
- output: bfloat16 [4096, 4096], P(('ctx', 'exp'))
Inputs may be any that keep to these rules, and one draw needn't show every extreme that they name: `route_ids`: each row names two different experts. In each aligned block of 32 rows no expert is named more than 8 times, a bound that some block reaches. `decay_rate`: Non-negative.
All inputs are finite; a program needn't handle non-finite values.
Results may differ from a plain program's by a relative error of at most 0.02.
Values may be sent and summed in bfloat16 or wider, within the bound.
A program may use at most 128 MiB of HBM per device.

v0:
```python
import jax
import jax.numpy as jnp
from jax import lax
from jax.sharding import PartitionSpec as P

PAIR = 2
eps_norm = 1e-05
top_precision = lax.Precision.HIGHEST


def entering(x, axis, join, neutral):
    place = lax.axis_index(axis)
    gathered = jax.tree.map(
        lambda a, kind: lax.all_gather(a.astype(kind), axis), x, (jnp.bfloat16, jnp.bfloat16)
    )
    state = jax.tree.map(lambda a, e: jnp.zeros_like(a) + jnp.asarray(e, a.dtype), x, neutral)

    def one(hop, state):
        return join(
            state,
            jax.tree.map(
                lambda a, own: lax.dynamic_index_in_dim(a, hop, 0, False).astype(own.dtype),
                gathered,
                x,
            ),
        )

    return lax.fori_loop(0, place, one, state)


def later_state(earlier, later):
    first_decay, first_state = earlier
    second_decay, second_state = later
    return (first_decay * second_decay, second_decay[:, None, None] * first_state + second_state)


def route_ranks(quarter_ids, experts):
    flattened = quarter_ids.reshape(-1)
    onehot = (flattened[:, None] == jnp.arange(experts, dtype=jnp.int32)[None, :]).astype(jnp.int32)
    running = jnp.cumsum(onehot, axis=0)
    rank_ids = jnp.sum(onehot * running, axis=1) - 1
    return (flattened, rank_ids)


def place_rows(normed, quarter_ids, experts, capacity):
    flattened, rank_ids = route_ranks(quarter_ids, experts)
    slot_ids = rank_ids * experts + flattened
    matches = (
        jnp.arange(capacity * experts, dtype=jnp.int32)[:, None] == slot_ids[None, :]
    ).astype(jnp.bfloat16)
    doubled = jnp.repeat(normed, quarter_ids.shape[1], axis=0)
    placed = jnp.dot(matches, doubled, preferred_element_type=jnp.float32).astype(jnp.bfloat16)
    return placed.reshape(capacity, experts, normed.shape[1])


def rms_rows(values, gain_vec):
    scaling = lax.rsqrt(jnp.mean(values * values, axis=1, keepdims=True) + eps_norm)
    return (values * scaling * gain_vec[None, :]).astype(jnp.bfloat16)


def local(
    inputs,
    gate_input,
    b_proj,
    c_proj,
    step_size,
    decay_rate,
    skip_gain,
    start_state,
    norm_gain,
    out_proj,
    residual,
    moe_gain,
    w_gate,
    w_up,
    w_down,
    route_ids,
    route_gates,
):
    tok_ctx = inputs.shape[0]
    head_count = step_size.shape[0]
    head_dim = inputs.shape[1] // head_count
    model_width = residual.shape[1]
    n_ctx = lax.axis_size("ctx")
    n_exp = lax.axis_size("exp")
    experts = n_ctx // PAIR
    tok_quarter = tok_ctx // n_exp
    capacity = 4 * tok_quarter // experts
    x_local = inputs.astype(jnp.float32).reshape(tok_ctx, head_count, head_dim)
    b_local = b_proj.astype(jnp.float32)
    c_local = c_proj.astype(jnp.float32)
    cumulative = jnp.cumsum(decay_rate, axis=1)
    span_total = cumulative[:, -1]
    sequence_indices = jnp.arange(tok_ctx, dtype=jnp.int32)
    causal = sequence_indices[:, None] >= sequence_indices[None, :]
    spread = jnp.where(causal[None], cumulative[:, :, None] - cumulative[:, None, :], 0.0)
    scores = jnp.dot(c_local, b_local.T, precision=top_precision)
    mixing = jnp.where(causal[None], jnp.exp(-spread), 0.0) * scores[None] * step_size[:, None, :]
    inside_part = jnp.einsum("hts,shp->thp", mixing, x_local, precision=top_precision)
    ending = jnp.exp(-(span_total[:, None] - cumulative)) * step_size
    local_state = jnp.einsum("hs,shp,sn->hpn", ending, x_local, b_local, precision=top_precision)
    prior_decay, prior_state = entering(
        (jnp.exp(-span_total), local_state),
        "ctx",
        later_state,
        (jnp.ones_like(span_total), jnp.zeros_like(local_state)),
    )
    incoming = prior_state + prior_decay[:, None, None] * start_state
    carried = (
        jnp.einsum("hpn,tn->thp", incoming, c_local, precision=top_precision)
        * jnp.exp(-cumulative).T[:, :, None]
    )
    ssm_out = inside_part + carried + skip_gain[None, :, None] * x_local
    gated_out = ssm_out.reshape(tok_ctx, head_count * head_dim) * jax.nn.silu(
        gate_input.astype(jnp.float32)
    )
    squares = lax.psum(jnp.sum(gated_out * gated_out, axis=1), "exp")
    scaling = lax.rsqrt(squares / (head_count * head_dim * n_exp) + eps_norm)
    normed_mix = (gated_out * scaling[:, None] * norm_gain[None, :]).astype(jnp.bfloat16)
    partial_value = jnp.dot(
        normed_mix,
        lax.all_gather(out_proj, "ctx", axis=1, tiled=True),
        preferred_element_type=jnp.float32,
    )
    gate_rows = w_gate[0]
    up_rows = w_up[0]
    down_rows = w_down[0]
    piece_width = gate_rows.shape[1]
    first_row = lax.axis_index("exp") * tok_quarter
    own_ids = lax.dynamic_slice_in_dim(route_ids, first_row, tok_quarter, 0)
    own_gates = lax.dynamic_slice_in_dim(route_gates, first_row, tok_quarter, 0)
    mixed_all = lax.psum(partial_value.astype(jnp.bfloat16), "exp").astype(jnp.float32)
    hidden_all = residual.astype(jnp.float32) + mixed_all
    moe_all = rms_rows(hidden_all, moe_gain)

    def place_quarter(quarter_rows, quarter_ids):
        return place_rows(quarter_rows, quarter_ids, experts, capacity)

    placed = jax.vmap(place_quarter)(
        moe_all.reshape(n_exp, tok_quarter, model_width),
        route_ids.reshape(n_exp, tok_quarter, route_ids.shape[1]),
    )
    placed = placed.reshape(n_exp * capacity, experts, model_width)
    outgoing = jnp.repeat(placed, PAIR, axis=1)
    arrived = lax.all_to_all(outgoing, "ctx", split_axis=1, concat_axis=1, tiled=True)
    flattened = arrived.reshape(-1, model_width)
    gate_val = jnp.dot(flattened, gate_rows, preferred_element_type=jnp.float32)
    up_val = jnp.dot(flattened, up_rows, preferred_element_type=jnp.float32)
    activated = (jax.nn.silu(gate_val) * up_val).astype(jnp.bfloat16)
    hidden = activated.reshape(arrived.shape[0], arrived.shape[1], piece_width)
    hidden_own = lax.dynamic_slice_in_dim(hidden_all, first_row, tok_quarter, 0)
    product = jnp.dot(
        hidden.reshape(-1, piece_width), down_rows, preferred_element_type=jnp.float32
    )
    rounded = lax.optimization_barrier(product.astype(jnp.bfloat16)).astype(jnp.float32)
    summed = lax.psum_scatter(
        rounded.reshape(lax.axis_size("exp") * capacity, hidden.shape[1], model_width).astype(
            jnp.bfloat16
        ),
        "exp",
        scatter_dimension=0,
        tiled=True,
    )
    halves = lax.all_to_all(summed, "ctx", split_axis=1, concat_axis=1, tiled=True)
    flattened, rank_ids = route_ranks(own_ids, experts)
    base_rows = rank_ids * n_ctx + flattened * PAIR
    fetch_rows = base_rows[:, None] + jnp.arange(PAIR, dtype=jnp.int32)[None, :]
    fetched = halves.reshape(capacity * n_ctx, model_width)[fetch_rows]
    expert_out = jnp.sum(fetched.astype(jnp.float32), axis=1)
    weighted = expert_out * own_gates.reshape(-1)[:, None]
    moe_out = jnp.sum(weighted.reshape(tok_quarter, -1, model_width), axis=1)
    return (hidden_own + moe_out).astype(jnp.bfloat16)


def solution(mesh):
    in_specs = (
        P("ctx", "exp"),
        P("ctx", "exp"),
        P("ctx", None),
        P("ctx", None),
        P("exp", "ctx"),
        P("exp", "ctx"),
        P("exp"),
        P("exp", None, None),
        P("exp"),
        P("exp", "ctx"),
        P("ctx", None),
        P(),
        P("ctx", None, "exp"),
        P("ctx", None, "exp"),
        P("ctx", "exp", None),
        P("ctx", None),
        P("ctx", None),
    )
    out_specs = P(("ctx", "exp"), None)
    return jax.shard_map(local, mesh=mesh, in_specs=in_specs, out_specs=out_specs, check_vma=False)
```

profile of v0, /device:TPU:1, one launch (start us, length us, event | category | flops | bytes accessed | tf_op | source)
XLA Modules:
  0.0 490.3 jit_solution(6920894452097007620)
XLA Ops:
  13.8 65.5 %all-reduce = bf16[512]{0:T(512)(128)(2,1)S(1)} all-reduce(bf16[512]{0:T(512)(128)(2,1)S(1)} %dynamic-update-slice), channel_id=2, replica_groups=mesh['ctx'=32,'exp'=4] {'ctx'}, use_global_device_ids=true, to_apply=%add | all-reduce | flops 512 | bytes 2048
  82.2 1.4 fusion.8
  84.1 8.4 %psum.14 = f32[128]{0:T(128)S(1)} all-reduce(f32[128]{0:T(128)S(1)} %multiply_reduce_fusion.2), channel_id=1, replica_groups=mesh['ctx'=32,'exp'=4] {'exp'}, use_global_device_ids=true, to_apply=%region_4.5 | all-reduce | flops 128 | bytes 1024 | tf_op jit(solution)/shard_map/psum | solution.py:117
  92.5 36.7 %all-gather.5.cloned.1.call-done = bf16[1024,4096]{1,0:T(8,128)(2,1)} async-done(((bf16[1024,128]{1,0:T(8,128)(2,1)}), bf16[1024,4096]{1,0:T(8,128)(2,1)}) %all-gather.5.cloned.1.call-update) | async-done | bytes 8388624 | tf_op jit(solution)/shard_map/all_gather | solution.py:122
  129.2 5.8 %convolution_convert_fusion.2 = bf16[128,4096]{1,0:T(8,128)(2,1)} fusion(bf16[1024,4096]{1,0:T(8,128)(2,1)} %all-gather.5.cloned.1.call-done, f32[1024]{0:T(1024)S(1)} %copy-done.12, f32[128]{0:T(128)S(1)} %add_rsqrt_fusion.1, f32[128,1024]{1,0:T(8,128)S(1)} %copy.62, bf16[128,1024]{1,0:T(8,128)(2,1)S(1)} %copy-done.6), kind=kOutput, calls=%fused_computation.10 | convolution fusion | flops 1075445760 | bytes 10228224 | tf_op jit(solution)/shard_map/dot_general | solution.py:120
  135.8 42.9 %all-reduce.3.cloned.1.call-done = bf16[128,4096]{1,0:T(8,128)(2,1)} async-done(((bf16[128,4096]{1,0:T(8,128)(2,1)}), bf16[128,4096]{1,0:T(8,128)(2,1)}) %all-reduce.3.cloned.1.call-update) | async-done | bytes 1048592 | tf_op jit(solution)/shard_map/psum | solution.py:132
  178.8 3.0 convert_add_fusion.1
  182.2 3.4 broadcast_in_dim.28
  185.7 2.7 reshape.157
  189.8 2.3 copy.64
  192.1 4.3 broadcast_in_dim.29
  196.3 105.0 %all_to_all.10 = bf16[32,32,4096]{2,0,1:T(8,128)(2,1)} all-to-all(bf16[32,32,4096]{2,0,1:T(8,128)(2,1)} %bitcast.66), channel_id=1, replica_groups=mesh['ctx'=32,'exp'=4] {'ctx'}, dimensions={1} | all-to-all | bytes 16777216 | tf_op jit(solution)/shard_map/all_to_all | solution.py:145
  301.4 11.3 %copy.65 = bf16[32,32,4096]{2,1,0:T(8,128)(2,1)} copy(bf16[32,32,4096]{2,0,1:T(8,128)(2,1)} %all_to_all.10) | data formatting | bytes 16777216 | tf_op jit(solution)/shard_map/all_to_all | solution.py:145
  312.7 13.0 %fusion.1 = f32[1024,896]{1,0:T(8,128)S(1)} fusion(bf16[1024,4096]{1,0:T(8,128)(2,1)} %bitcast.68, bf16[1,4096,896]{2,1,0:T(8,128)(2,1)} %param.32), kind=kOutput, calls=%fused_computation.5 | convolution fusion | flops 7516192768 | bytes 19398656 | tf_op jit(solution)/shard_map/dot_general | solution.py:148
  325.8 9.2 %multiply_convert_fusion = bf16[1024,896]{1,0:T(8,128)(2,1)S(1)} fusion(f32[1024,896]{1,0:T(8,128)S(1)} %fusion.1, bf16[1024,4096]{1,0:T(8,128)(2,1)S(1)} %bitcast.69, bf16[1,4096,896]{2,1,0:T(8,128)(2,1)S(1)} %bitcast.78), kind=kOutput, calls=%fused_computation.11 | convolution fusion | flops 7521697792 | bytes 21233664 | tf_op jit(solution)/shard_map/dot_general | solution.py:147
  335.0 11.2 %convolution_convert_fusion = bf16[1024,4096]{1,0:T(8,128)(2,1)} fusion(bf16[1024,896]{1,0:T(8,128)(2,1)S(1)} %multiply_convert_fusion, bf16[1,896,4096]{2,1,0:T(8,128)(2,1)S(1)} %bitcast.80), kind=kOutput, calls=%fused_computation.3 | convolution fusion | flops 7520387072 | bytes 17563648 | tf_op jit(solution)/shard_map/dot_general | solution.py:152
  346.2 11.3 %copy.74 = bf16[4,8,32,4096]{3,1,2,0:T(8,128)(2,1)} copy(bf16[4,8,32,4096]{3,2,1,0:T(8,128)(2,1)} %bitcast.70) | data formatting | bytes 16777216
  357.5 77.8 %reduce-scatter.4.cloned.1.call-done = bf16[8,131072]{1,0:T(8,128)(2,1)} async-done(((bf16[32,131072]{1,0:T(8,128)(2,1)}), bf16[8,131072]{1,0:T(8,128)(2,1)}) %reduce-scatter.4.cloned.1.call-update) | async-done | bytes 2097168
  435.3 8.1 %all-to-all-start.1 = ((bf16[8,32,4096]{2,0,1:T(8,128)(2,1)}), bf16[8,32,4096]{2,0,1:T(8,128)(2,1)}, u32[]{:S(2)}, u32[]{:S(2)}) async-start(bf16[8,32,4096]{2,0,1:T(8,128)(2,1)} %bitcast.72), calls=%async_computation.1 | async-start | bytes 4194304 | tf_op jit(solution)/shard_map/all_to_all | solution.py:164
  444.5 27.1 %all-to-all-done.1 = bf16[8,32,4096]{2,0,1:T(8,128)(2,1)} async-done(((bf16[8,32,4096]{2,0,1:T(8,128)(2,1)}), bf16[8,32,4096]{2,0,1:T(8,128)(2,1)}, u32[]{:S(2)}, u32[]{:S(2)}) %all-to-all-start.1) | async-done | bytes 2097184 | tf_op jit(solution)/shard_map/all_to_all | solution.py:164
  471.6 2.7 copy.67
  476.9 2.7 reduce_sum.60
  480.2 1.4 multiply_reduce_fusion.1
  481.7 1.8 add_convert_fusion
  (92 shorter events, 17.8 us)
Async XLA Ops:
  6.5 3.1 copy-start
  6.5 73.9 %all-gather.7.cloned.1.call-start = ((), (), s32[]{:S(2)}) async-start(), calls=%async_computation.5 | async-start | bytes 8650752 | tf_op jit(solution)/shard_map/all_gather | solution.py:14
  10.7 118.4 %all-gather.5.cloned.1.call-start = ((), (), s32[]{:S(2)}) async-start(), calls=%async_computation.3 | async-start | bytes 8650752 | tf_op jit(solution)/shard_map/all_gather | solution.py:122
  11.5 167.3 %all-reduce.3.cloned.1.call-start = ((), (), s32[]{:S(2)}) async-start(), calls=%async_computation.4 | async-start | bytes 2097152 | tf_op jit(solution)/shard_map/psum | solution.py:132
  80.3 1.4 copy-start.5
  80.3 1.4 copy-start.7
  80.5 1.7 copy-start.9
  80.5 1.7 copy-start.13
  81.7 2.1 copy-start.6
  81.7 47.5 %copy-start.12 = (f32[1024]{0:T(1024)S(1)}, f32[1024]{0:T(1024)}, u32[]{:S(2)}) copy-start(f32[1024]{0:T(1024)} %param.27) | copy-start | bytes 12292
  92.5 42.6 %copy-start.10 = (s32[128,2]{0,1:T(2,128)S(1)}, s32[128,2]{0,1:T(2,128)}, u32[]{:S(2)}) copy-start(s32[128,2]{0,1:T(2,128)} %param.34) | copy-start | bytes 3076
  92.5 86.3 %copy-start.3 = (bf16[128,4096]{1,0:T(8,128)(2,1)S(1)}, bf16[128,4096]{1,0:T(8,128)(2,1)}, u32[]{:S(2)}) copy-start(bf16[128,4096]{1,0:T(8,128)(2,1)} %param.29) | copy-start | bytes 3145732
  135.0 46.8 %copy-start.8 = (f32[4096]{0:T(1024)S(1)}, f32[4096]{0:T(1024)}, u32[]{:S(2)}) copy-start(f32[4096]{0:T(1024)} %param.30) | copy-start | bytes 49156
  135.1 300.3 %reduce-scatter.4.cloned.1.call-start = ((), (), s32[]{:S(2)}) async-start(), calls=%async_computation.6 | async-start | bytes 10485760
  178.8 3.0 copy-start.4
  301.4 24.4 %slice-start = ((s8[7340032]{0:T(1024)(128)(4,1)}), s8[3145728]{0:T(1024)(128)(4,1)S(1)}, s32[]{:S(2)}) async-start(s8[7340032]{0:T(1024)(128)(4,1)} %bitcast.77), calls=%async_computation.7 | async-start | bytes 6291456
  312.7 13.0 %copy-start.2 = (bf16[32,32,4096]{2,1,0:T(8,128)(2,1)S(1)}, bf16[32,32,4096]{2,1,0:T(8,128)(2,1)}, u32[]{:S(2)}) copy-start(bf16[32,32,4096]{2,1,0:T(8,128)(2,1)} %copy.65) | copy-start | bytes 25165828
  312.7 13.0 %slice-start.1 = ((s8[7340032]{0:T(1024)(128)(4,1)}), s8[4194304]{0:T(1024)(128)(4,1)S(1)}, s32[]{:S(2)}) async-start(s8[7340032]{0:T(1024)(128)(4,1)} %bitcast.77), calls=%async_computation.8 | async-start | bytes 8388608
  312.7 22.2 %slice-start.2 = ((s8[7340032]{0:T(1024)(128)(4,1)}), s8[4194304]{0:T(1024)(128)(4,1)S(1)}, s32[]{:S(2)}) async-start(s8[7340032]{0:T(1024)(128)(4,1)} %bitcast.79), calls=%async_computation.9 | async-start | bytes 8388608
  325.8 9.2 %slice-start.3 = ((s8[7340032]{0:T(1024)(128)(4,1)}), s8[3145728]{0:T(1024)(128)(4,1)S(1)}, s32[]{:S(2)}) async-start(s8[7340032]{0:T(1024)(128)(4,1)} %bitcast.79), calls=%async_computation.10 | async-start | bytes 6291456
  357.5 86.8 %copy-start.11 = (f32[128,2]{0,1:T(2,128)S(1)}, f32[128,2]{0,1:T(2,128)}, u32[]{:S(2)}) copy-start(f32[128,2]{0,1:T(2,128)} %param.35) | copy-start | bytes 3076
  435.3 36.3 %all-to-all-start.1 = ((bf16[8,32,4096]{2,0,1:T(8,128)(2,1)}), bf16[8,32,4096]{2,0,1:T(8,128)(2,1)}, u32[]{:S(2)}, u32[]{:S(2)}) async-start(bf16[8,32,4096]{2,0,1:T(8,128)(2,1)} %bitcast.72), calls=%async_computation.1 | async-start | bytes 4194304 | tf_op jit(solution)/shard_map/all_to_all | solution.py:164
  475.5 8.0 %copy-start.1 = (bf16[128,128]{1,0:T(8,128)(2,1)S(1)}, bf16[128,128]{1,0:T(8,128)(2,1)}, u32[]{:S(2)}) copy-start(bf16[128,128]{1,0:T(8,128)(2,1)} %param.21) | copy-start | bytes 98308
Sparse Core Ops, SparseCore 0:
  10.9 56.8 all-gather.6
  69.9 59.2 all-gather.4
  135.2 43.5 all-reduce.2
  357.7 77.6 reduce-scatter.3
where the time goes:
time: 500 us; the launch traced here: 490 us
  waiting for transfers between devices  185 us (37%)
  blocking collectives  179 us (36%)
  local copies, waits for them, and re-layouts  45.3 us (9%)
  matrix products  44.4 us (9%)
  between operations  14.4 us (3%)
  other arithmetic  13.7 us (3%)
  starting transfers between devices  8.24 us (2%)
    all_to_all x1, blocking collectives, local(): lax.all_to_all(outgoing, 'ctx', split_axis=1, concat_axis=1, tiled=True)  105 us
    unnamed x5, waiting for transfers between devices  78.5 us
    unnamed x1, blocking collectives  65.5 us
    psum x1, waiting for transfers between devices, local(): lax.psum(partial_value.astype(jnp.bfloat16), 'exp').astype(jnp.float32)  42.9 us
    all_gather x1, waiting for transfers between devices, local(): lax.all_gather(out_proj, 'ctx', axis=1, tiled=True)  36.7 us
    all_to_all x1, waiting for transfers between devices, local(): lax.all_to_all(summed, 'ctx', split_axis=1, concat_axis=1, tiled=True)  27.1 us
    unnamed x42, local copies, waits for them, and re-layouts  14.1 us
    dot_general x1, matrix products, local(): up_val = jnp.dot(flattened, up_rows, preferred_element_type=jnp.float32)  13 us
  transfers between devices with their start and end apart: 5, of which 4 were waited for; matrix products, arithmetic and copies ran while one was open for 2% of the time, Pallas kernels for 0%

commit v1 on v0

--- a/solution.py
+++ b/solution.py
@@ -129,7 +129,9 @@
     first_row = lax.axis_index("exp") * tok_quarter
     own_ids = lax.dynamic_slice_in_dim(route_ids, first_row, tok_quarter, 0)
     own_gates = lax.dynamic_slice_in_dim(route_gates, first_row, tok_quarter, 0)
-    mixed_all = lax.psum(partial_value.astype(jnp.bfloat16), "exp").astype(jnp.float32)
+    mixed_all = (
+        lax.all_gather(partial_value.astype(jnp.bfloat16), "exp").sum(axis=0).astype(jnp.float32)
+    )
     hidden_all = residual.astype(jnp.float32) + mixed_all
     moe_all = rms_rows(hidden_all, moe_gain)
 

time: 500 us -> 500 us (level)
    all_gather x0 -> x1, waiting for transfers between devices: none -> 46.5 us  [local(): lax.all_gather(partial_value.astype(jnp.bfloat16), 'exp').sum(axis=0)]
    psum x1 -> x0, waiting for transfers between devices: 42.9 us -> none  [local(): lax.psum(partial_value.astype(jnp.bfloat16), 'exp').astype(jnp.float32)]
    unnamed x42 -> x40, local copies, waits for them, and re-layouts: 14.1 us -> 14.1 us
where the time goes in v1:
time: 500 us; the launch traced here: 494 us
  waiting for transfers between devices  188 us (38%)
  blocking collectives  178 us (36%)
  local copies, waits for them, and re-layouts  45.3 us (9%)
  matrix products  44.1 us (9%)
  other arithmetic  15.5 us (3%)
  between operations  14.4 us (3%)
  starting transfers between devices  8.55 us (2%)
    all_to_all x1, blocking collectives, local(): lax.all_to_all(outgoing, 'ctx', split_axis=1, concat_axis=1, tiled=True)  104 us
    unnamed x5, waiting for transfers between devices  78 us
    unnamed x1, blocking collectives  65.5 us
    all_gather x1, waiting for transfers between devices, local(): lax.all_gather(partial_value.astype(jnp.bfloat16), 'exp').sum(axis=0)  46.5 us
    all_gather x1, waiting for transfers between devices, local(): lax.all_gather(out_proj, 'ctx', axis=1, tiled=True)  36.7 us
    all_to_all x1, waiting for transfers between devices, local(): lax.all_to_all(summed, 'ctx', split_axis=1, concat_axis=1, tiled=True)  27.1 us
    unnamed x40, local copies, waits for them, and re-layouts  14.1 us
    dot_general x1, matrix products, local(): up_val = jnp.dot(flattened, up_rows, preferred_element_type=jnp.float32)  12.7 us
  transfers between devices with their start and end apart: 5, of which 4 were waited for; matrix products, arithmetic and copies ran while one was open for 2% of the time, Pallas kernels for 0%

profile of v1, /device:TPU:1, one launch (start us, length us, event | category | flops | bytes accessed | tf_op | source)
XLA Modules:
  0.0 494.0 jit_solution(18223204004579888819)
XLA Ops:
  13.8 65.5 %all-reduce = bf16[512]{0:T(512)(128)(2,1)S(1)} all-reduce(bf16[512]{0:T(512)(128)(2,1)S(1)} %dynamic-update-slice), channel_id=2, replica_groups=mesh['ctx'=32,'exp'=4] {'ctx'}, use_global_device_ids=true, to_apply=%add | all-reduce | flops 512 | bytes 2048
  84.1 8.4 %psum.7 = f32[128]{0:T(128)S(1)} all-reduce(f32[128]{0:T(128)S(1)} %multiply_reduce_fusion.2), channel_id=1, replica_groups=mesh['ctx'=32,'exp'=4] {'exp'}, use_global_device_ids=true, to_apply=%region_4.5 | all-reduce | flops 128 | bytes 1024 | tf_op jit(solution)/shard_map/psum | solution.py:117
  92.5 36.7 %all-gather.7.cloned.1.call-done = bf16[1024,4096]{1,0:T(8,128)(2,1)} async-done(((bf16[1024,128]{1,0:T(8,128)(2,1)}), bf16[1024,4096]{1,0:T(8,128)(2,1)}) %all-gather.7.cloned.1.call-update) | async-done | bytes 8388624 | tf_op jit(solution)/shard_map/all_gather | solution.py:122
  129.2 5.8 %convolution_convert_fusion.2 = bf16[128,4096]{1,0:T(8,128)(2,1)} fusion(bf16[1024,4096]{1,0:T(8,128)(2,1)} %all-gather.7.cloned.1.call-done, f32[1024]{0:T(1024)S(1)} %copy-done.11, f32[128]{0:T(128)S(1)} %add_rsqrt_fusion.1, f32[128,1024]{1,0:T(8,128)S(1)} %copy.62, bf16[128,1024]{1,0:T(8,128)(2,1)S(1)} %copy-done.5), kind=kOutput, calls=%fused_computation.10 | convolution fusion | flops 1075445760 | bytes 10228224 | tf_op jit(solution)/shard_map/dot_general | solution.py:120
  136.1 46.5 %all-gather.11.cloned.1.call-done = bf16[512,4096]{1,0:T(8,128)(2,1)} async-done(((bf16[128,4096]{1,0:T(8,128)(2,1)}), bf16[512,4096]{1,0:T(8,128)(2,1)}) %all-gather.11.cloned.1.call-update) | async-done | bytes 4194320 | tf_op jit(solution)/shard_map/all_gather | solution.py:133
  182.6 3.1 reduce_sum.69
  185.7 1.7 convert_add_fusion.1
  187.8 3.4 broadcast_in_dim.28
  191.3 2.7 reshape.157
  195.4 2.3 copy.64
  197.7 4.3 broadcast_in_dim.29
  202.0 103.9 %all_to_all.10 = bf16[32,32,4096]{2,0,1:T(8,128)(2,1)} all-to-all(bf16[32,32,4096]{2,0,1:T(8,128)(2,1)} %bitcast.67), channel_id=1, replica_groups=mesh['ctx'=32,'exp'=4] {'ctx'}, dimensions={1} | all-to-all | bytes 16777216 | tf_op jit(solution)/shard_map/all_to_all | solution.py:147
  305.9 11.3 %copy.65 = bf16[32,32,4096]{2,1,0:T(8,128)(2,1)} copy(bf16[32,32,4096]{2,0,1:T(8,128)(2,1)} %all_to_all.10) | data formatting | bytes 16777216 | tf_op jit(solution)/shard_map/all_to_all | solution.py:147
  317.2 12.7 %fusion.1 = f32[1024,896]{1,0:T(8,128)S(1)} fusion(bf16[1024,4096]{1,0:T(8,128)(2,1)} %bitcast.69, bf16[1,4096,896]{2,1,0:T(8,128)(2,1)} %param.32), kind=kOutput, calls=%fused_computation.5 | convolution fusion | flops 7516192768 | bytes 19398656 | tf_op jit(solution)/shard_map/dot_general | solution.py:150
  329.9 9.2 %multiply_convert_fusion = bf16[1024,896]{1,0:T(8,128)(2,1)S(1)} fusion(f32[1024,896]{1,0:T(8,128)S(1)} %fusion.1, bf16[1024,4096]{1,0:T(8,128)(2,1)S(1)} %bitcast.70, bf16[1,4096,896]{2,1,0:T(8,128)(2,1)S(1)} %bitcast.80), kind=kOutput, calls=%fused_computation.11 | convolution fusion | flops 7521697792 | bytes 21233664 | tf_op jit(solution)/shard_map/dot_general | solution.py:149
  339.1 11.3 %convolution_convert_fusion = bf16[1024,4096]{1,0:T(8,128)(2,1)} fusion(bf16[1024,896]{1,0:T(8,128)(2,1)S(1)} %multiply_convert_fusion, bf16[1,896,4096]{2,1,0:T(8,128)(2,1)S(1)} %bitcast.82), kind=kOutput, calls=%fused_computation.3 | convolution fusion | flops 7520387072 | bytes 17563648 | tf_op jit(solution)/shard_map/dot_general | solution.py:154
  350.4 11.3 %copy.74 = bf16[4,8,32,4096]{3,1,2,0:T(8,128)(2,1)} copy(bf16[4,8,32,4096]{3,2,1,0:T(8,128)(2,1)} %bitcast.71) | data formatting | bytes 16777216
  361.7 77.2 %reduce-scatter.4.cloned.1.call-done = bf16[8,131072]{1,0:T(8,128)(2,1)} async-done(((bf16[32,131072]{1,0:T(8,128)(2,1)}), bf16[8,131072]{1,0:T(8,128)(2,1)}) %reduce-scatter.4.cloned.1.call-update) | async-done | bytes 2097168
  439.0 8.1 %all-to-all-start.1 = ((bf16[8,32,4096]{2,0,1:T(8,128)(2,1)}), bf16[8,32,4096]{2,0,1:T(8,128)(2,1)}, u32[]{:S(2)}, u32[]{:S(2)}) async-start(bf16[8,32,4096]{2,0,1:T(8,128)(2,1)} %bitcast.74), calls=%async_computation.1 | async-start | bytes 4194304 | tf_op jit(solution)/shard_map/all_to_all | solution.py:166
  448.2 27.1 %all-to-all-done.1 = bf16[8,32,4096]{2,0,1:T(8,128)(2,1)} async-done(((bf16[8,32,4096]{2,0,1:T(8,128)(2,1)}), bf16[8,32,4096]{2,0,1:T(8,128)(2,1)}, u32[]{:S(2)}, u32[]{:S(2)}) %all-to-all-start.1) | async-done | bytes 2097184 | tf_op jit(solution)/shard_map/all_to_all | solution.py:166
  475.3 2.7 copy.67
  480.6 2.7 reduce_sum.73
  483.9 1.4 multiply_reduce_fusion.1
  485.3 1.8 add_convert_fusion
  (91 shorter events, 19.5 us)
Async XLA Ops:
  6.5 3.1 copy-start
  6.5 73.9 %all-gather.9.cloned.1.call-start = ((), (), s32[]{:S(2)}) async-start(), calls=%async_computation.4 | async-start | bytes 8650752 | tf_op jit(solution)/shard_map/all_gather | solution.py:14
  10.7 118.4 %all-gather.7.cloned.1.call-start = ((), (), s32[]{:S(2)}) async-start(), calls=%async_computation.3 | async-start | bytes 8650752 | tf_op jit(solution)/shard_map/all_gather | solution.py:122
  11.5 171.1 %all-gather.11.cloned.1.call-start = ((), (), s32[]{:S(2)}) async-start(), calls=%async_computation.5 | async-start | bytes 5242880 | tf_op jit(solution)/shard_map/all_gather | solution.py:133
  80.3 1.4 copy-start.4
  80.3 1.4 copy-start.6
  80.5 1.7 copy-start.8
  80.5 1.7 copy-start.12
  81.7 2.1 copy-start.5
  81.7 47.5 %copy-start.11 = (f32[1024]{0:T(1024)S(1)}, f32[1024]{0:T(1024)}, u32[]{:S(2)}) copy-start(f32[1024]{0:T(1024)} %param.27) | copy-start | bytes 12292
  92.5 42.9 %copy-start.9 = (s32[128,2]{0,1:T(2,128)S(1)}, s32[128,2]{0,1:T(2,128)}, u32[]{:S(2)}) copy-start(s32[128,2]{0,1:T(2,128)} %param.34) | copy-start | bytes 3076
  135.0 50.7 %copy-start.3 = (bf16[128,4096]{1,0:T(8,128)(2,1)S(1)}, bf16[128,4096]{1,0:T(8,128)(2,1)}, u32[]{:S(2)}) copy-start(bf16[128,4096]{1,0:T(8,128)(2,1)} %param.29) | copy-start | bytes 3145732
  135.1 303.9 %reduce-scatter.4.cloned.1.call-start = ((), (), s32[]{:S(2)}) async-start(), calls=%async_computation.6 | async-start | bytes 10485760
  182.6 4.8 copy-start.7
  305.9 24.0 %slice-start = ((s8[7340032]{0:T(1024)(128)(4,1)}), s8[3145728]{0:T(1024)(128)(4,1)S(1)}, s32[]{:S(2)}) async-start(s8[7340032]{0:T(1024)(128)(4,1)} %bitcast.79), calls=%async_computation.7 | async-start | bytes 6291456
  317.2 12.7 %copy-start.2 = (bf16[32,32,4096]{2,1,0:T(8,128)(2,1)S(1)}, bf16[32,32,4096]{2,1,0:T(8,128)(2,1)}, u32[]{:S(2)}) copy-start(bf16[32,32,4096]{2,1,0:T(8,128)(2,1)} %copy.65) | copy-start | bytes 25165828
  317.2 12.7 %slice-start.1 = ((s8[7340032]{0:T(1024)(128)(4,1)}), s8[4194304]{0:T(1024)(128)(4,1)S(1)}, s32[]{:S(2)}) async-start(s8[7340032]{0:T(1024)(128)(4,1)} %bitcast.79), calls=%async_computation.8 | async-start | bytes 8388608
  317.2 21.9 %slice-start.2 = ((s8[7340032]{0:T(1024)(128)(4,1)}), s8[4194304]{0:T(1024)(128)(4,1)S(1)}, s32[]{:S(2)}) async-start(s8[7340032]{0:T(1024)(128)(4,1)} %bitcast.81), calls=%async_computation.9 | async-start | bytes 8388608
  329.9 9.2 %slice-start.3 = ((s8[7340032]{0:T(1024)(128)(4,1)}), s8[3145728]{0:T(1024)(128)(4,1)S(1)}, s32[]{:S(2)}) async-start(s8[7340032]{0:T(1024)(128)(4,1)} %bitcast.81), calls=%async_computation.10 | async-start | bytes 6291456
  361.7 86.3 %copy-start.10 = (f32[128,2]{0,1:T(2,128)S(1)}, f32[128,2]{0,1:T(2,128)}, u32[]{:S(2)}) copy-start(f32[128,2]{0,1:T(2,128)} %param.35) | copy-start | bytes 3076
  439.0 36.3 %all-to-all-start.1 = ((bf16[8,32,4096]{2,0,1:T(8,128)(2,1)}), bf16[8,32,4096]{2,0,1:T(8,128)(2,1)}, u32[]{:S(2)}, u32[]{:S(2)}) async-start(bf16[8,32,4096]{2,0,1:T(8,128)(2,1)} %bitcast.74), calls=%async_computation.1 | async-start | bytes 4194304 | tf_op jit(solution)/shard_map/all_to_all | solution.py:166
  479.2 8.0 %copy-start.1 = (bf16[128,128]{1,0:T(8,128)(2,1)S(1)}, bf16[128,128]{1,0:T(8,128)(2,1)}, u32[]{:S(2)}) copy-start(bf16[128,128]{1,0:T(8,128)(2,1)} %param.21) | copy-start | bytes 98308
Sparse Core Ops, SparseCore 0:
  10.9 56.8 all-gather.8
  69.9 59.2 all-gather.6
  135.2 47.3 all-gather.10
  361.8 77.0 reduce-scatter.3
